TPU v7x, 256 devices: a whole 4x4x8 slice. The times are simulated.
256 devices in a mesh: wide: 32 (over y, x, core), narrow: 8 (over z).
Axes of the slice: x: 4, y: 4, z: 8, core: 2. Of those that a mesh axis runs over, the one named last changes fastest.
Arguments:
- constraint_rows: bfloat16 [512, 256, 1024], P(None, ('wide', 'narrow')), may hold values from -1 to 1
- metric: bfloat16 [1024, 1024], replicated, may hold values from -8 to 8, as said below
Outputs:
- factored: float32 [512, 256, 8, 128], P(None, 'wide', 'narrow')
Inputs may be any that keep to these rules, and one draw needn't show every extreme that they name: `metric`: symmetric and positive definite.
All inputs are finite; a program needn't handle non-finite values.
Results may differ from a plain program's by a relative error of at most 0.0052.
Values may be sent and summed in bfloat16 or wider, within the bound.
No kernel may reach another device: no remote copies, remote signals or barrier semaphores. Data moves between devices by JAX's collectives and lax.ppermute only.
A program may use at most 64 MiB of HBM per device.

v0:
```python
import jax
import jax.numpy as jnp
from jax import lax
from jax.sharding import PartitionSpec as P

P_SIZE = 1024
PB = 256
NPANEL = 2


def left_solve(factor_low, right_side):
    return jax.scipy.linalg.solve_triangular(factor_low, right_side, lower=True)


def strip_major(schur_slab, strips):
    row_count = schur_slab.shape[0]
    strip_len = schur_slab.shape[1] // strips
    reordered = schur_slab.reshape(row_count, strip_len, strips).transpose(0, 2, 1)
    return reordered.reshape(row_count, 1, strips, strip_len)


def local(constraint_rows, metric):
    groups = lax.axis_size(("wide", "narrow"))
    strips = lax.axis_size("narrow")
    row_count = constraint_rows.shape[0]
    panel_depth = P_SIZE // groups
    block_rows = PB // groups
    flat_rows = constraint_rows[:, 0, :]
    projected = jnp.dot(flat_rows, metric, preferred_element_type=jnp.float32).astype(jnp.bfloat16)
    gram_cols = jnp.einsum(
        "rn,kmn->rkm",
        projected,
        lax.all_gather(constraint_rows[:panel_depth], ("wide", "narrow"), axis=1, tiled=True),
        preferred_element_type=jnp.float32,
    )
    schur_slab = (gram_cols * gram_cols).reshape(row_count, P_SIZE)
    grid_block = lax.all_to_all(
        strip_major(schur_slab, strips), "narrow", split_axis=2, concat_axis=1, tiled=True
    )
    strip_len = P_SIZE // strips
    grid_rows = row_count * strips
    narrow_panel = PB // strips
    own_strip = lax.axis_index("narrow")
    flat_block = grid_block.reshape(grid_rows, strip_len)
    for panel_number in range(NPANEL):
        col_begin = panel_number * PB
        row_begin = col_begin // groups
        strip_begin = col_begin // strips
        strip_end = strip_begin + narrow_panel
        own_rows = flat_block.reshape(row_count, strips, strip_len)[
            row_begin : row_begin + block_rows, :, strip_begin:
        ]
        shared = lax.all_gather(own_rows, "wide", axis=1, tiled=True)
        shared = shared.reshape(PB, strip_len - strip_begin)
        diag_strip, row_strip = (
            lax.all_gather(shared[:, :narrow_panel], "narrow", axis=1, tiled=True),
            lax.all_gather(flat_block[:, strip_begin:strip_end], "narrow", axis=1, tiled=True),
        )
        diag_block = diag_strip.reshape(PB, strips, narrow_panel).transpose(0, 2, 1).reshape(PB, PB)
        panel_cols = (
            row_strip.reshape(grid_rows, strips, narrow_panel)
            .transpose(0, 2, 1)
            .reshape(grid_rows, PB)
        )
        factor_low = jnp.linalg.cholesky(diag_block)
        upper_part = left_solve(factor_low, shared[:, narrow_panel:])
        column = left_solve(factor_low, panel_cols.T).T
        trailing = flat_block[:, strip_end:] - jnp.dot(
            column, upper_part, precision=lax.Precision.HIGHEST
        )
        own_cols = lax.dynamic_index_in_dim(
            column.reshape(grid_rows, narrow_panel, strips), own_strip, 2, keepdims=False
        )
        flat_block = jnp.concatenate([flat_block[:, :strip_begin], own_cols, trailing], axis=1)
    return flat_block.reshape(row_count, strips, 1, strip_len)


def solution(mesh):
    placed = (P(None, ("wide", "narrow"), None), P())
    return jax.shard_map(
        local,
        mesh=mesh,
        in_specs=placed,
        out_specs=P(None, "wide", "narrow", None),
        check_vma=False,
    )
```

profile of v0, /device:TPU:4, one launch (start us, length us, event | category | flops | bytes accessed | tf_op | source)
XLA Modules:
  0.0 463.7 jit_solution(18273028846116087548)
XLA Ops:
  8.1 110.0 %all-gather.6.cloned.1.call-done = bf16[4,256,1024]{2,0,1:T(4,128)(2,1)} async-done(((bf16[4,1,1024]{2,0,1:T(4,128)(2,1)}), bf16[4,256,1024]{2,0,1:T(4,128)(2,1)}) %all-gather.6.cloned.1.call-update) | async-done | bytes 2097168 | tf_op jit(solution)/shard_map/all_gather | solution.py:33
  118.1 5.7 %fusion.8 = f32[512,4,256]{0,2,1:T(8,128)} fusion(bf16[4,256,1024]{2,0,1:T(4,128)(2,1)} %all-gather.6.cloned.1.call-done, bf16[1024,1024]{1,0:T(8,128)(2,1)S(1)} %copy-done, bf16[512,1,1024]{2,0,1:T(8,128)(2,1)} %param.5), kind=kOutput, calls=%fused_computation.22 | convolution fusion | flops 2148532224 | bytes 7340032 | tf_op jit(solution)/shard_map/rn,kmn->rkm/dot_general | solution.py:30
  125.8 56.3 %all_to_all.4 = f32[512,1,8,128]{3,1,0,2:T(1,128)S(1)} all-to-all(f32[512,1,8,128]{3,1,0,2:T(1,128)S(1)} %bitcast.153), channel_id=1, replica_groups=mesh['wide'=32,'narrow'=8] {'narrow'}, dimensions={2} | all-to-all | bytes 4194304 | tf_op jit(solution)/shard_map/all_to_all | solution.py:37
  186.8 23.0 %all-gather = f32[1,1,256,128]{3,2,1,0:T(8,128)S(1)} all-gather(f32[1,1,8,128]{3,2,1,0:T(8,128)S(1)} %bitcast.150), channel_id=2, replica_groups=mesh['wide'=32,'narrow'=8] {'wide'}, dimensions={2}, use_global_device_ids=true | all-gather | bytes 135168 | tf_op jit(solution)/shard_map/all_gather | solution.py:53
  210.1 26.7 %all_gather.23 = f32[256,256]{0,1:T(8,128)S(1)} all-gather(f32[256,32]{0,1:T(8,128)S(1)} %copy.64), channel_id=1, replica_groups=mesh['wide'=32,'narrow'=8] {'narrow'}, dimensions={1}, use_global_device_ids=true | all-gather | bytes 294912 | tf_op jit(solution)/shard_map/all_gather | solution.py:56
  237.3 11.7 %cholesky.130 = f32[128,128]{1,0:T(8,128)S(1)} custom-call(f32[128,128]{1,0:T(8,128)S(1)} %cholesky.194), custom_call_target="Cholesky" | custom-call | tf_op jit(solution)/shard_map/jit(cholesky)/cholesky | solution.py:65
  249.1 9.8 %custom-call.23 = f32[1,128,128]{1,2,0:T(8,128)S(1)} custom-call(f32[1,128,128]{2,1,0:T(8,128)S(1)} %get-tuple-element.66), custom_call_target="InvertDiagBlocksLowerTriangular" | custom-call | tf_op jit(solution)/shard_map/jit(cholesky)/cholesky | solution.py:65
  259.4 11.7 %cholesky.147 = f32[128,128]{1,0:T(8,128)S(1)} custom-call(f32[128,128]{1,0:T(8,128)S(1)} %convolution_subtract_fusion.5), custom_call_target="Cholesky" | custom-call | tf_op jit(solution)/shard_map/jit(cholesky)/cholesky | solution.py:65
  273.2 3.9 while.6
  277.1 19.7 %custom-call.24 = f32[2,128,128]{1,2,0:T(8,128)S(1)} custom-call(f32[2,128,128]{2,1,0:T(8,128)S(1)} %get-tuple-element.37), custom_call_target="InvertDiagBlocksLowerTriangular" | custom-call | tf_op jit(solution)/shard_map/jit(_solve_triangular)/triangular_solve | solution.py:12
  296.8 2.1 copy.83
  299.8 4.6 copy.99
  310.3 2.7 convolution_subtract_fusion.2
  316.0 24.0 %all-gather.1 = f32[256,96]{1,0:T(8,128)S(1)} all-gather(f32[8,96]{1,0:T(8,128)S(1)} %copy.73), channel_id=3, replica_groups=mesh['wide'=32,'narrow'=8] {'wide'}, dimensions={0}, use_global_device_ids=true | all-gather | bytes 101376 | tf_op jit(solution)/shard_map/all_gather | solution.py:53
  340.2 26.5 %all_gather.26 = f32[256,256]{0,1:T(8,128)S(1)} all-gather(f32[256,32]{0,1:T(8,128)S(1)} %copy.85), channel_id=1, replica_groups=mesh['wide'=32,'narrow'=8] {'narrow'}, dimensions={1}, use_global_device_ids=true | all-gather | bytes 294912 | tf_op jit(solution)/shard_map/all_gather | solution.py:56
  367.2 11.7 %cholesky.164 = f32[128,128]{1,0:T(8,128)S(1)} custom-call(f32[128,128]{1,0:T(8,128)S(1)} %cholesky.197), custom_call_target="Cholesky" | custom-call | tf_op jit(solution)/shard_map/jit(cholesky)/cholesky | solution.py:65
  378.9 9.8 %custom-call.25 = f32[1,128,128]{1,2,0:T(8,128)S(1)} custom-call(f32[1,128,128]{2,1,0:T(8,128)S(1)} %get-tuple-element.62), custom_call_target="InvertDiagBlocksLowerTriangular" | custom-call | tf_op jit(solution)/shard_map/jit(cholesky)/cholesky | solution.py:65
  389.3 11.7 %cholesky.181 = f32[128,128]{1,0:T(8,128)S(1)} custom-call(f32[128,128]{1,0:T(8,128)S(1)} %convolution_subtract_fusion.4), custom_call_target="Cholesky" | custom-call | tf_op jit(solution)/shard_map/jit(cholesky)/cholesky | solution.py:65
  403.6 3.9 while.7
  407.5 19.7 %custom-call.26 = f32[2,128,128]{1,2,0:T(8,128)S(1)} custom-call(f32[2,128,128]{2,1,0:T(8,128)S(1)} %get-tuple-element.38), custom_call_target="InvertDiagBlocksLowerTriangular" | custom-call | tf_op jit(solution)/shard_map/jit(_solve_triangular)/triangular_solve | solution.py:12
  427.2 2.0 fusion.1
  432.5 4.6 copy.98
  444.4 2.9 convolution_subtract_fusion.3
  451.5 5.5 %pad_maximum_fusion.4 = f32[512,8,1,128]{3,1,0,2:T(8,128)} fusion(f32[512,8,1,64]{3,1,0,2:T(8,128)} %bitcast.154, f32[512,8,1,32]{3,1,0,2:T(8,128)} %bitcast.152, f32[512,8,1,32]{3,1,0,2:T(8,128)} %bitcast.151), kind=kLoop, calls=%fused_computation.18 | loop fusion | flops 1048576 | bytes 4194304 | tf_op jit(solution)/shard_map/concatenate | solution.py:74
  (97 shorter events, 44.8 us)
Async XLA Ops:
  6.5 111.6 %copy-start = (bf16[1024,1024]{1,0:T(8,128)(2,1)S(1)}, bf16[1024,1024]{1,0:T(8,128)(2,1)}, u32[]{:S(2)}) copy-start(bf16[1024,1024]{1,0:T(8,128)(2,1)} %param.6) | copy-start | bytes 6291460
  6.5 111.6 %all-gather.6.cloned.1.call-start = ((), (), s32[]{:S(2)}) async-start(), calls=%async_computation.1 | async-start | bytes 2105344 | tf_op jit(solution)/shard_map/all_gather | solution.py:33
  8.0 291.7 %all-gather.8.cloned.1.call-start = ((), (), s32[]{:S(2)}) async-start(), calls=%async_computation.2 | async-start | bytes 4718592 | tf_op jit(solution)/shard_map/all_gather | solution.py:57
  182.1 1.3 copy-start.3
  184.8 247.6 %all-gather.10.cloned.1.call-start = ((), (), s32[]{:S(2)}) async-start(), calls=%async_computation.3 | async-start | bytes 4718592 | tf_op jit(solution)/shard_map/all_gather | solution.py:57
  184.9 1.9 slice-start
  237.0 59.8 %copy-start.4 = (f32[4096,96]{1,0:T(8,128)S(1)}, f32[4096,96]{1,0:T(8,128)}, u32[]{:S(2)}) copy-start(f32[4096,96]{1,0:T(8,128)} %slice.153) | copy-start | bytes 4718596
  308.3 2.0 copy-start.7
  310.3 2.8 copy-start.2
  313.0 1.1 copy-start.5
  442.9 1.4 copy-start.6
  451.5 5.5 %copy-start.1 = (bf16[1024,1024]{1,0:T(8,128)(2,1)S(1)}, bf16[1024,1024]{1,0:T(8,128)(2,1)}, u32[]{:S(2)}) copy-start(bf16[1024,1024]{1,0:T(8,128)(2,1)} %param.6) | copy-start | bytes 6291460
Sparse Core Ops, SparseCore 0:
  11.1 107.0 all-gather.5
  184.9 53.2 all-gather.7
  315.2 53.6 all-gather.9
where the time goes:
time: 469 us; the launch traced here: 464 us
  blocking collectives  157 us (33%)
  other arithmetic  116 us (25%)
  waiting for transfers between devices  110 us (23%)
  local copies, waits for them, and re-layouts  38.8 us (8%)
  matrix products  25.5 us (5%)
  between operations  16.2 us (3%)
    all_gather x1, waiting for transfers between devices, local(): lax.all_gather(constraint_rows[:panel_depth], ('wide', 'narrow'), axis=1,...  110 us
    another operation x13, other arithmetic, local(): factor_low = jnp.linalg.cholesky(diag_block)  68.6 us
    all_to_all x1, blocking collectives, local(): lax.all_to_all(strip_major(schur_slab, strips), 'narrow', split_axis=2, c...  56.3 us
    all_gather x2, blocking collectives, local(): lax.all_gather(shared[:, :narrow_panel], 'narrow', axis=1, tiled=True)  53.2 us
    all_gather x2, blocking collectives, local(): shared = lax.all_gather(own_rows, 'wide', axis=1, tiled=True)  47 us
    another operation x5, other arithmetic, left_solve(): return jax.scipy.linalg.solve_triangular(factor_low, right_side, lower=True)  39.4 us
    another operation x12, matrix products, left_solve(): return jax.scipy.linalg.solve_triangular(factor_low, right_side, lower=True)  13.2 us
  transfers between devices with their start and end apart: 3, of which 1 were waited for; matrix products, arithmetic and copies ran while one was open for 28% of the time, Pallas kernels for 0%

commit v1 on v0

--- a/solution.py
+++ b/solution.py
@@ -50,7 +50,9 @@
         own_rows = flat_block.reshape(row_count, strips, strip_len)[
             row_begin : row_begin + block_rows, :, strip_begin:
         ]
-        shared = lax.all_gather(own_rows, "wide", axis=1, tiled=True)
+        shared = jnp.concatenate(
+            lax.all_to_all(jnp.stack([own_rows] * lax.axis_size("wide")), "wide", 0, 0), axis=1
+        )
         shared = shared.reshape(PB, strip_len - strip_begin)
         diag_strip, row_strip = (
             lax.all_gather(shared[:, :narrow_panel], "narrow", axis=1, tiled=True),

time: 469 us -> 442 us (0.942)
  blocking collectives: 157 us -> 110 us
  starting transfers between devices: 0.09 us -> 14.2 us
    all_gather x2 -> x0, blocking collectives: 47 us -> none  [local(): shared = lax.all_gather(own_rows, 'wide', axis=1, tiled=True)]
    all_to_all x0 -> x2, starting transfers between devices: none -> 14.1 us  [local(): lax.all_to_all(jnp.stack([own_rows] * lax.axis_size('wide')), 'wide', 0, 0)]
  transfers between devices with their start and end apart: 3 -> 5, of which waited for: 1 -> 3; matrix products, arithmetic and copies ran while one was open for 28% -> 30% of each run, Pallas kernels for 0% -> 0%
where the time goes in v1:
time: 442 us; the launch traced here: 436 us
  other arithmetic  117 us (26%)
  waiting for transfers between devices  112 us (25%)
  blocking collectives  110 us (25%)
  local copies, waits for them, and re-layouts  40.9 us (9%)
  matrix products  25.5 us (6%)
  between operations  16.4 us (4%)
  starting transfers between devices  14.2 us (3%)
    all_gather x1, waiting for transfers between devices, local(): lax.all_gather(constraint_rows[:panel_depth], ('wide', 'narrow'), axis=1,...  110 us
    another operation x13, other arithmetic, local(): factor_low = jnp.linalg.cholesky(diag_block)  68.6 us
    all_to_all x1, blocking collectives, local(): lax.all_to_all(strip_major(schur_slab, strips), 'narrow', split_axis=2, c...  56.3 us
    all_gather x2, blocking collectives, local(): lax.all_gather(shared[:, :narrow_panel], 'narrow', axis=1, tiled=True)  53.3 us
    another operation x5, other arithmetic, left_solve(): return jax.scipy.linalg.solve_triangular(factor_low, right_side, lower=True)  40 us
    all_to_all x2, starting transfers between devices, local(): lax.all_to_all(jnp.stack([own_rows] * lax.axis_size('wide')), 'wide', 0, 0)  14.1 us
    another operation x12, matrix products, left_solve(): return jax.scipy.linalg.solve_triangular(factor_low, right_side, lower=True)  13.2 us
  transfers between devices with their start and end apart: 5, of which 3 were waited for; matrix products, arithmetic and copies ran while one was open for 30% of the time, Pallas kernels for 0%

profile of v1, /device:TPU:4, one launch (start us, length us, event | category | flops | bytes accessed | tf_op | source)
XLA Modules:
  0.0 435.6 jit_solution(18240408538784316189)
XLA Ops:
  8.1 110.0 %all-gather.4.cloned.1.call-done = bf16[4,256,1024]{2,0,1:T(4,128)(2,1)} async-done(((bf16[4,1,1024]{2,0,1:T(4,128)(2,1)}), bf16[4,256,1024]{2,0,1:T(4,128)(2,1)}) %all-gather.4.cloned.1.call-update) | async-done | bytes 2097168 | tf_op jit(solution)/shard_map/all_gather | solution.py:33
  118.1 5.7 %fusion.8 = f32[512,4,256]{0,2,1:T(8,128)} fusion(bf16[4,256,1024]{2,0,1:T(4,128)(2,1)} %all-gather.4.cloned.1.call-done, bf16[1024,1024]{1,0:T(8,128)(2,1)S(1)} %copy-done, bf16[512,1,1024]{2,0,1:T(8,128)(2,1)} %param.5), kind=kOutput, calls=%fused_computation.22 | convolution fusion | flops 2148532224 | bytes 7340032 | tf_op jit(solution)/shard_map/rn,kmn->rkm/dot_general | solution.py:30
  125.8 56.3 %all_to_all.19 = f32[512,1,8,128]{3,1,0,2:T(1,128)S(1)} all-to-all(f32[512,1,8,128]{3,1,0,2:T(1,128)S(1)} %bitcast.156), channel_id=1, replica_groups=mesh['wide'=32,'narrow'=8] {'narrow'}, dimensions={2} | all-to-all | bytes 4194304 | tf_op jit(solution)/shard_map/all_to_all | solution.py:37
  185.5 7.3 %all-to-all-start.1 = ((f32[32,1,8,128]{3,2,1,0:T(8,128)}), f32[32,1,8,128]{3,2,1,0:T(8,128)S(1)}, u32[]{:S(2)}, u32[]{:S(2)}) async-start(f32[32,1,8,128]{3,2,1,0:T(8,128)} %stack.7), calls=%async_computation.1 | async-start | bytes 262144 | tf_op jit(solution)/shard_map/all_to_all | solution.py:54
  194.8 2.8 copy.67
  198.6 26.7 %all_gather.16 = f32[256,256]{0,1:T(8,128)S(1)} all-gather(f32[256,32]{0,1:T(8,128)S(1)} %copy.48), channel_id=1, replica_groups=mesh['wide'=32,'narrow'=8] {'narrow'}, dimensions={1}, use_global_device_ids=true | all-gather | bytes 294912 | tf_op jit(solution)/shard_map/all_gather | solution.py:58
  225.8 11.7 %cholesky.130 = f32[128,128]{1,0:T(8,128)S(1)} custom-call(f32[128,128]{1,0:T(8,128)S(1)} %cholesky.194), custom_call_target="Cholesky" | custom-call | tf_op jit(solution)/shard_map/jit(cholesky)/cholesky | solution.py:67
  237.5 9.8 %custom-call.23 = f32[1,128,128]{1,2,0:T(8,128)S(1)} custom-call(f32[1,128,128]{2,1,0:T(8,128)S(1)} %get-tuple-element.66), custom_call_target="InvertDiagBlocksLowerTriangular" | custom-call | tf_op jit(solution)/shard_map/jit(cholesky)/cholesky | solution.py:67
  247.9 11.7 %cholesky.147 = f32[128,128]{1,0:T(8,128)S(1)} custom-call(f32[128,128]{1,0:T(8,128)S(1)} %convolution_subtract_fusion.5), custom_call_target="Cholesky" | custom-call | tf_op jit(solution)/shard_map/jit(cholesky)/cholesky | solution.py:67
  261.7 4.0 while.6
  265.7 20.1 %custom-call.24 = f32[2,128,128]{1,2,0:T(8,128)S(1)} custom-call(f32[2,128,128]{2,1,0:T(8,128)S(1)} %get-tuple-element.37), custom_call_target="InvertDiagBlocksLowerTriangular" | custom-call | tf_op jit(solution)/shard_map/jit(_solve_triangular)/triangular_solve | solution.py:12
  286.6 4.6 %copy.82 = f32[4096,32,8]{0,2,1:T(8,128)S(1)} copy(f32[4096,32,8]{0,1,2:T(8,128)} %bitcast.159) | data formatting | bytes 8388608 | tf_op jit(solution)/shard_map/transpose | solution.py:64
  297.1 2.7 convolution_subtract_fusion.2
  303.6 6.8 %all-to-all-start.2 = ((f32[32,1,8,96]{3,2,1,0:T(8,128)}), f32[32,1,8,96]{3,2,1,0:T(8,128)S(1)}, u32[]{:S(2)}, u32[]{:S(2)}) async-start(f32[32,1,8,96]{3,2,1,0:T(8,128)} %stack.8), calls=%async_computation.2 | async-start | bytes 262144 | tf_op jit(solution)/shard_map/all_to_all | solution.py:54
  310.4 2.0 fusion.1
  316.0 26.6 %all_gather.18 = f32[256,256]{0,1:T(8,128)S(1)} all-gather(f32[256,32]{0,1:T(8,128)S(1)} %copy.58), channel_id=1, replica_groups=mesh['wide'=32,'narrow'=8] {'narrow'}, dimensions={1}, use_global_device_ids=true | all-gather | bytes 294912 | tf_op jit(solution)/shard_map/all_gather | solution.py:58
  343.0 11.7 %cholesky.164 = f32[128,128]{1,0:T(8,128)S(1)} custom-call(f32[128,128]{1,0:T(8,128)S(1)} %cholesky.197), custom_call_target="Cholesky" | custom-call | tf_op jit(solution)/shard_map/jit(cholesky)/cholesky | solution.py:67
  354.8 9.8 %custom-call.25 = f32[1,128,128]{1,2,0:T(8,128)S(1)} custom-call(f32[1,128,128]{2,1,0:T(8,128)S(1)} %get-tuple-element.62), custom_call_target="InvertDiagBlocksLowerTriangular" | custom-call | tf_op jit(solution)/shard_map/jit(cholesky)/cholesky | solution.py:67
  365.1 11.7 %cholesky.181 = f32[128,128]{1,0:T(8,128)S(1)} custom-call(f32[128,128]{1,0:T(8,128)S(1)} %convolution_subtract_fusion.4), custom_call_target="Cholesky" | custom-call | tf_op jit(solution)/shard_map/jit(cholesky)/cholesky | solution.py:67
  379.6 4.1 while.7
  383.7 19.9 %custom-call.26 = f32[2,128,128]{1,2,0:T(8,128)S(1)} custom-call(f32[2,128,128]{2,1,0:T(8,128)S(1)} %get-tuple-element.38), custom_call_target="InvertDiagBlocksLowerTriangular" | custom-call | tf_op jit(solution)/shard_map/jit(_solve_triangular)/triangular_solve | solution.py:12
  404.4 4.6 %copy.81 = f32[4096,8,32]{0,1,2:T(8,128)S(1)} copy(f32[4096,8,32]{0,2,1:T(8,128)} %bitcast.158) | data formatting | bytes 8388608 | tf_op jit(solution)/shard_map/reshape | solution.py:63
  416.3 2.9 convolution_subtract_fusion.3
  423.4 5.5 %pad_maximum_fusion.4 = f32[512,8,1,128]{3,1,0,2:T(8,128)} fusion(f32[512,8,1,64]{3,1,0,2:T(8,128)} %bitcast.157, f32[512,8,1,32]{3,1,0,2:T(8,128)} %bitcast.155, f32[512,8,1,32]{3,1,0,2:T(8,128)} %bitcast.154), kind=kLoop, calls=%fused_computation.18 | loop fusion | flops 1048576 | bytes 4194304 | tf_op jit(solution)/shard_map/concatenate | solution.py:76
  (99 shorter events, 48.2 us)
Async XLA Ops:
  6.5 111.6 %copy-start = (bf16[1024,1024]{1,0:T(8,128)(2,1)S(1)}, bf16[1024,1024]{1,0:T(8,128)(2,1)}, u32[]{:S(2)}) copy-start(bf16[1024,1024]{1,0:T(8,128)(2,1)} %param.6) | copy-start | bytes 6291460
  6.5 111.6 %all-gather.4.cloned.1.call-start = ((), (), s32[]{:S(2)}) async-start(), calls=%async_computation.3 | async-start | bytes 2105344 | tf_op jit(solution)/shard_map/all_gather | solution.py:33
  8.0 278.6 %all-gather.6.cloned.1.call-start = ((), (), s32[]{:S(2)}) async-start(), calls=%async_computation.4 | async-start | bytes 4718592 | tf_op jit(solution)/shard_map/all_gather | solution.py:59
  182.1 1.3 copy-start.3
  183.4 1.4 slice-start
  185.5 12.9 %all-to-all-start.1 = ((f32[32,1,8,128]{3,2,1,0:T(8,128)}), f32[32,1,8,128]{3,2,1,0:T(8,128)S(1)}, u32[]{:S(2)}, u32[]{:S(2)}) async-start(f32[32,1,8,128]{3,2,1,0:T(8,128)} %stack.7), calls=%async_computation.1 | async-start | bytes 262144 | tf_op jit(solution)/shard_map/all_to_all | solution.py:54
  192.8 211.6 %all-gather.8.cloned.1.call-start = ((), (), s32[]{:S(2)}) async-start(), calls=%async_computation.5 | async-start | bytes 4718592 | tf_op jit(solution)/shard_map/all_gather | solution.py:59
  295.1 2.0 copy-start.6
  297.1 2.8 copy-start.2
  299.9 1.2 copy-start.4
  303.6 12.2 %all-to-all-start.2 = ((f32[32,1,8,96]{3,2,1,0:T(8,128)}), f32[32,1,8,96]{3,2,1,0:T(8,128)S(1)}, u32[]{:S(2)}, u32[]{:S(2)}) async-start(f32[32,1,8,96]{3,2,1,0:T(8,128)} %stack.8), calls=%async_computation.2 | async-start | bytes 262144 | tf_op jit(solution)/shard_map/all_to_all | solution.py:54
  414.9 1.4 copy-start.5
  423.4 5.5 %copy-start.1 = (bf16[1024,1024]{1,0:T(8,128)(2,1)S(1)}, bf16[1024,1024]{1,0:T(8,128)(2,1)}, u32[]{:S(2)}) copy-start(bf16[1024,1024]{1,0:T(8,128)(2,1)} %param.6) | copy-start | bytes 6291460
Sparse Core Ops, SparseCore 0:
  11.1 107.0 all-gather.3
  184.9 53.5 all-gather.5
  302.1 53.6 all-gather.7
